TPU v7x, 32 devices: a whole 2x2x4 slice. The times are simulated.
32 devices in a mesh: shot: 8 (over y, x, core), pair: 4 (over z).
Axes of the slice: x: 2, y: 2, z: 4, core: 2. Of those that a mesh axis runs over, the one named last changes fastest.
Arguments:
- spectra: bfloat16 [2, 128, 128, 1024], P(None, 'shot', None, 'pair'), may hold values from -6 to 6
- shot_weight: float32 [128], P('shot'), may hold values from 0.5 to 2
Outputs:
- virtual_gather: bfloat16 [2, 128, 1024, 1024], P(None, 'shot', 'pair')
All inputs are finite; a program needn't handle non-finite values.
Results may differ from a plain program's by a relative error of at most 0.0054.
Values may be sent and summed in bfloat16 or wider, within the bound.
A program may use at most 128 MiB of HBM per device.

v0:
```python
import jax
import jax.numpy as jnp
from jax import lax
from jax.sharding import PartitionSpec as P


def gram_block(row_data, column_data, factor):
    swapped = jnp.stack([-row_data[1], row_data[0]])
    left_side = jnp.stack([row_data, swapped])
    product = jnp.einsum(
        "ocsfa,csfb->ofab", left_side, column_data, preferred_element_type=jnp.float32
    )
    return product * factor


def shards(spectra, shot_weight):
    scaled = (spectra.astype(jnp.float32) * shot_weight[None, :, None, None]).astype(jnp.bfloat16)
    by_freq = lax.all_to_all(scaled, "shot", split_axis=2, concat_axis=1, tiled=True)
    total_shots = by_freq.shape[1]
    factor = total_shots ** (-0.5)
    full_rows = gram_block(by_freq, lax.all_gather(by_freq, "pair", axis=3, tiled=True), factor)
    return full_rows.astype(jnp.bfloat16)


def solution(mesh):
    return jax.shard_map(
        shards,
        mesh=mesh,
        in_specs=(P(None, "shot", None, "pair"), P("shot")),
        out_specs=P(None, "shot", "pair", None),
        check_vma=False,
    )
```

profile of v0, /device:TPU:0, one launch (start us, length us, event | category | flops | bytes accessed | tf_op | source)
XLA Modules:
  0.0 237.3 jit_solution(6709182819881926623)
XLA Ops:
  6.5 0.0 all-gather.2.cloned.1.call-start
  6.5 2.8 %multiply_convert_fusion = bf16[2,16,128,256]{3,1,0,2:T(8,128)(2,1)S(1)} fusion(bf16[2,16,128,256]{3,2,1,0:T(8,128)(2,1)} %param.2, f32[16]{0:T(128)} %param.3), kind=kLoop, calls=%fused_computation.7 | loop fusion | flops 3145728 | bytes 4194368 | tf_op jit(solution)/shard_map/convert_element_type | solution.py:17
  9.4 31.6 %all_to_all.18 = bf16[2,16,128,256]{3,1,0,2:T(8,128)(2,1)S(1)} all-to-all(bf16[2,16,128,256]{3,1,0,2:T(8,128)(2,1)S(1)} %multiply_convert_fusion), channel_id=1, replica_groups=mesh['shot'=8,'pair'=4] {'shot'}, dimensions={2} | all-to-all | bytes 4194304 | tf_op jit(solution)/shard_map/all_to_all | solution.py:18
  40.9 2.5 %copy.20 = bf16[2,8,16,16,256]{4,3,2,1,0:T(8,128)(2,1)} copy(bf16[2,8,16,16,256]{4,2,0,3,1:T(8,128)(2,1)S(1)} %bitcast.25) | data formatting | bytes 4194304 | tf_op jit(solution)/shard_map/all_to_all | solution.py:18
  43.4 4.6 %copy.21 = bf16[2,128,16,256]{1,3,0,2:T(8,128)(2,1)} copy(bf16[2,128,16,256]{3,2,1,0:T(8,128)(2,1)} %bitcast.28) | data formatting | bytes 4194304 | tf_op jit(solution)/shard_map/all_to_all | solution.py:18
  48.0 0.0 all-gather.2.cloned.1.call-update
  48.0 1.6 copy.22
  49.6 1.2 copy.19
  50.8 0.1 slice_negate_fusion
  50.9 0.0 copy-start
  50.9 0.6 copy.23
  51.5 0.6 copy.24
  52.1 1.5 maximum_bitcast_fusion
  53.6 143.5 %all-gather.2.cloned.1.call-done = bf16[2,128,16,1024]{1,3,0,2:T(8,128)(2,1)} async-done(((bf16[2,128,16,256]{1,3,0,2:T(8,128)(2,1)}), bf16[2,128,16,1024]{1,3,0,2:T(8,128)(2,1)}) %all-gather.2.cloned.1.call-update) | async-done | bytes 8388624 | tf_op jit(solution)/shard_map/all_gather | solution.py:21
  197.2 0.0 copy-done
  197.2 11.0 %fusion.1 = bf16[2,16,256,1024]{2,3,0,1:T(8,128)(2,1)} fusion(bf16[2,128,16,1024]{1,3,0,2:T(8,128)(2,1)} %all-gather.2.cloned.1.call-done, bf16[1,2,128,16,256]{4,2,1,0,3:T(8,128)(2,1)} %maximum_bitcast_fusion, bf16[1,2,128,16,256]{4,2,1,0,3:T(8,128)(2,1)S(1)} %bitcast.31), kind=kOutput, calls=%fused_computation.2 | convolution fusion | flops 4320133120 | bytes 29360128 | tf_op jit(solution)/shard_map/ocsfa,csfb->ofab/dot_general | solution.py:10
  208.1 22.4 %copy.25 = bf16[2,16,256,1024]{3,2,1,0:T(8,128)(2,1)} copy(bf16[2,16,256,1024]{2,3,0,1:T(8,128)(2,1)} %fusion.1) | data formatting | bytes 33554432 | tf_op jit(solution)/shard_map/convert_element_type | solution.py:22
Async XLA Ops:
  6.5 190.6 %all-gather.2.cloned.1.call-start = ((), (), s32[]{:S(2)}) async-start(), calls=%async_computation.1 | async-start | bytes 10485760 | tf_op jit(solution)/shard_map/all_gather | solution.py:21
  50.9 146.2 %copy-start = (bf16[2,8,16,16,256]{4,2,1,0,3:T(8,128)(2,1)S(1)}, bf16[2,8,16,16,256]{4,2,1,0,3:T(8,128)(2,1)}, u32[]{:S(2)}) copy-start(bf16[2,8,16,16,256]{4,2,1,0,3:T(8,128)(2,1)} %copy.22) | copy-start | bytes 6291460
Sparse Core Ops, SparseCore 0:
  48.1 148.9 all-gather.1
where the time goes:
time: 238 us; the launch traced here: 237 us
  waiting for transfers between devices  144 us (61%)
  local copies, waits for them, and re-layouts  33.4 us (14%)
  blocking collectives  31.6 us (13%)
  between operations  13.4 us (6%)
  matrix products  11 us (5%)
  other arithmetic  4.48 us (2%)
    all_gather x1, waiting for transfers between devices, shards(): lax.all_gather(by_freq, 'pair', axis=3, tiled=True)  144 us
    all_to_all x1, blocking collectives, shards(): lax.all_to_all(scaled, 'shot', split_axis=2, concat_axis=1, tiled=True)  31.6 us
    convert_element_type x1, local copies, waits for them, and re-layouts, shards(): return full_rows.astype(jnp.bfloat16)  22.4 us
    dot_general x1, matrix products, gram_block(): jnp.einsum('ocsfa,csfb->ofab', left_side, column_data, preferred_element_...  11 us
    all_to_all x4, local copies, waits for them, and re-layouts, shards(): lax.all_to_all(scaled, 'shot', split_axis=2, concat_axis=1, tiled=True)  9.82 us
  transfers between devices with their start and end apart: 1, of which 1 were waited for; matrix products, arithmetic and copies ran while one was open for 2% of the time, Pallas kernels for 0%

commit v1 on v0

--- a/solution.py
+++ b/solution.py
@@ -2,6 +2,11 @@
 import jax.numpy as jnp
 from jax import lax
 from jax.sharding import PartitionSpec as P
+
+
+def swapped_in(x, name, dim):
+    sent = jnp.stack([x] * lax.axis_size(name))
+    return jnp.concatenate(lax.all_to_all(sent, name, 0, 0), axis=dim)
 
 
 def gram_block(row_data, column_data, factor):
@@ -18,7 +23,7 @@
     by_freq = lax.all_to_all(scaled, "shot", split_axis=2, concat_axis=1, tiled=True)
     total_shots = by_freq.shape[1]
     factor = total_shots ** (-0.5)
-    full_rows = gram_block(by_freq, lax.all_gather(by_freq, "pair", axis=3, tiled=True), factor)
+    full_rows = gram_block(by_freq, swapped_in(by_freq, "pair", 3), factor)
     return full_rows.astype(jnp.bfloat16)
 
 

time: 238 us -> 277 us (1.16)
  waiting for transfers between devices: 144 us -> 179 us
  between operations: 13.4 us -> 0.04 us
  local copies, waits for them, and re-layouts: 33.4 us -> 44.7 us
  starting transfers between devices: 0.01 us -> 5.63 us
    all_to_all x0 -> x1, waiting for transfers between devices: none -> 179 us  [swapped_in(): return jnp.concatenate(lax.all_to_all(sent, name, 0, 0), axis=dim)]
    all_gather x1 -> x0, waiting for transfers between devices: 144 us -> none  [shards(): lax.all_gather(by_freq, 'pair', axis=3, tiled=True)]
    another operation x0 -> x2, local copies, waits for them, and re-layouts: none -> 9.47 us  [swapped_in(): sent = jnp.stack([x] * lax.axis_size(name))]
    reshape x0 -> x1, local copies, waits for them, and re-layouts: none -> 8.04 us  [swapped_in(): return jnp.concatenate(lax.all_to_all(sent, name, 0, 0), axis=dim)]
    all_to_all x4 -> x2, local copies, waits for them, and re-layouts: 9.82 us -> 3.45 us  [shards(): lax.all_to_all(scaled, 'shot', split_axis=2, concat_axis=1, tiled=True)]
    all_to_all x0 -> x1, starting transfers between devices: none -> 5.63 us  [swapped_in(): return jnp.concatenate(lax.all_to_all(sent, name, 0, 0), axis=dim)]
  transfers between devices with their start and end apart: 1 -> 1, of which waited for: 1 -> 1; matrix products, arithmetic and copies ran while one was open for 2% -> 1% of each run, Pallas kernels for 0% -> 0%
where the time goes in v1:
time: 277 us; the launch traced here: 276 us
  waiting for transfers between devices  179 us (65%)
  local copies, waits for them, and re-layouts  44.7 us (16%)
  blocking collectives  31.6 us (11%)
  matrix products  11.6 us (4%)
  starting transfers between devices  5.63 us (2%)
  other arithmetic  3.17 us (1%)
    all_to_all x1, waiting for transfers between devices, swapped_in(): return jnp.concatenate(lax.all_to_all(sent, name, 0, 0), axis=dim)  179 us
    all_to_all x1, blocking collectives, shards(): lax.all_to_all(scaled, 'shot', split_axis=2, concat_axis=1, tiled=True)  31.6 us
    convert_element_type x1, local copies, waits for them, and re-layouts, shards(): return full_rows.astype(jnp.bfloat16)  22.4 us
    dot_general x1, matrix products, gram_block(): jnp.einsum('ocsfa,csfb->ofab', left_side, column_data, preferred_element_...  11.6 us
    another operation x2, local copies, waits for them, and re-layouts, swapped_in(): sent = jnp.stack([x] * lax.axis_size(name))  9.47 us
    reshape x1, local copies, waits for them, and re-layouts, swapped_in(): return jnp.concatenate(lax.all_to_all(sent, name, 0, 0), axis=dim)  8.04 us
    all_to_all x1, starting transfers between devices, swapped_in(): return jnp.concatenate(lax.all_to_all(sent, name, 0, 0), axis=dim)  5.63 us
  transfers between devices with their start and end apart: 1, of which 1 were waited for; matrix products, arithmetic and copies ran while one was open for 1% of the time, Pallas kernels for 0%

profile of v1, /device:TPU:0, one launch (start us, length us, event | category | flops | bytes accessed | tf_op | source)
XLA Modules:
  0.0 275.9 jit_solution(15598127306906102214)
XLA Ops:
  0.0 2.8 %multiply_convert_fusion = bf16[2,16,128,256]{3,1,0,2:T(8,128)(2,1)S(1)} fusion(bf16[2,16,128,256]{3,2,1,0:T(8,128)(2,1)} %param.2, f32[16]{0:T(128)} %param.3), kind=kLoop, calls=%fused_computation.6 | loop fusion | flops 3145728 | bytes 4194368 | tf_op jit(solution)/shard_map/convert_element_type | solution.py:22
  2.8 31.6 %all_to_all.20 = bf16[2,16,128,256]{3,1,0,2:T(8,128)(2,1)S(1)} all-to-all(bf16[2,16,128,256]{3,1,0,2:T(8,128)(2,1)S(1)} %multiply_convert_fusion), channel_id=1, replica_groups=mesh['shot'=8,'pair'=4] {'shot'}, dimensions={2} | all-to-all | bytes 4194304 | tf_op jit(solution)/shard_map/all_to_all | solution.py:23
  34.4 0.0 copy-start
  34.4 1.3 copy-done
  35.8 0.3 copy.19
  36.0 2.4 copy.9
  38.4 7.1 %stack.23 = bf16[4,2,128,16,256]{2,4,1,3,0:T(8,128)(2,1)} broadcast(bf16[2,128,16,256]{1,3,0,2:T(8,128)(2,1)} %copy.9), dimensions={1,2,3,4} | broadcast | bytes 10485760 | tf_op jit(solution)/shard_map/stack | solution.py:8
  45.5 5.6 %all-to-all-start.1 = ((bf16[4,2,128,16,256]{2,4,1,3,0:T(8,128)(2,1)}), bf16[4,2,128,16,256]{2,4,1,3,0:T(8,128)(2,1)}, u32[]{:S(2)}, u32[]{:S(2)}) async-start(bf16[4,2,128,16,256]{2,4,1,3,0:T(8,128)(2,1)} %stack.23), calls=%async_computation.1 | async-start | bytes 16777216 | tf_op jit(solution)/shard_map/all_to_all | solution.py:9
  51.1 3.2 %copy.11 = bf16[2,8,16,16,256]{4,2,1,0,3:T(8,128)(2,1)} copy(bf16[2,8,16,16,256]{4,2,0,3,1:T(8,128)(2,1)} %bitcast.32) | data formatting | bytes 4194304 | tf_op jit(solution)/shard_map/all_to_all | solution.py:23
  54.3 0.1 slice_negate_fusion
  54.5 0.2 maximum_bitcast_fusion
  54.7 179.3 %all-to-all-done.1 = bf16[4,2,128,16,256]{2,4,1,3,0:T(8,128)(2,1)} async-done(((bf16[4,2,128,16,256]{2,4,1,3,0:T(8,128)(2,1)}), bf16[4,2,128,16,256]{2,4,1,3,0:T(8,128)(2,1)}, u32[]{:S(2)}, u32[]{:S(2)}) %all-to-all-start.1) | async-done | bytes 8388640 | tf_op jit(solution)/shard_map/all_to_all | solution.py:9
  233.9 0.0 copy-start.1
  233.9 8.0 %copy.10 = bf16[2,128,16,4,256]{1,4,3,0,2:T(8,128)(2,1)} copy(bf16[2,128,16,4,256]{1,4,0,2,3:T(8,128)(2,1)} %bitcast.3) | data formatting | bytes 16777216 | tf_op jit(solution)/shard_map/reshape | solution.py:9
  242.0 0.0 copy-done.1
  242.0 11.6 %fusion.1 = bf16[2,16,256,1024]{2,3,0,1:T(8,128)(2,1)} fusion(bf16[2,128,16,1024,1]{1,3,0,4,2:T(8,128)(2,1)} %bitcast.33, bf16[1,2,128,16,256]{4,2,1,0,3:T(8,128)(2,1)S(1)} %maximum_bitcast_fusion, bf16[1,2,128,16,256]{4,2,1,0,3:T(8,128)(2,1)S(1)} %bitcast.36), kind=kOutput, calls=%fused_computation.2 | convolution fusion | flops 4320133120 | bytes 29360128 | tf_op jit(solution)/shard_map/ocsfa,csfb->ofab/dot_general | solution.py:15
  253.5 22.4 %copy.12 = bf16[2,16,256,1024]{3,2,1,0:T(8,128)(2,1)} copy(bf16[2,16,256,1024]{2,3,0,1:T(8,128)(2,1)} %fusion.1) | data formatting | bytes 33554432 | tf_op jit(solution)/shard_map/convert_element_type | solution.py:27
Async XLA Ops:
  34.4 1.4 copy-start
  45.5 188.4 %all-to-all-start.1 = ((bf16[4,2,128,16,256]{2,4,1,3,0:T(8,128)(2,1)}), bf16[4,2,128,16,256]{2,4,1,3,0:T(8,128)(2,1)}, u32[]{:S(2)}, u32[]{:S(2)}) async-start(bf16[4,2,128,16,256]{2,4,1,3,0:T(8,128)(2,1)} %stack.23), calls=%async_computation.1 | async-start | bytes 16777216 | tf_op jit(solution)/shard_map/all_to_all | solution.py:9
  233.9 8.0 %copy-start.1 = (bf16[2,8,16,16,256]{4,2,1,0,3:T(8,128)(2,1)S(1)}, bf16[2,8,16,16,256]{4,2,1,0,3:T(8,128)(2,1)}, u32[]{:S(2)}) copy-start(bf16[2,8,16,16,256]{4,2,1,0,3:T(8,128)(2,1)} %copy.11) | copy-start | bytes 6291460
